TPU v7x, 32 devices: a whole 2x2x4 slice. The times are simulated.
32 devices in a mesh: dp: 8 (over z, y), chan: 4 (over x, core).
Axes of the slice: x: 2, y: 2, z: 4, core: 2. Of those that a mesh axis runs over, the one named last changes fastest.
Arguments:
- activations: bfloat16 [8, 16, 64, 1024], P('dp', None, None, 'chan'), may hold values from -60 to 60
- cotangent: bfloat16 [8, 16, 64, 1024], P('dp', None, None, 'chan'), may hold values from -6 to 6
- dw_kernel: float32 [49, 1024], P(None, 'chan'), may hold values from -0.875 to 0.875
- norm_gain: float32 [4, 1024], P(None, 'chan'), may hold values from 0.1 to 1.9
- norm_bias: float32 [4, 1024], P(None, 'chan'), may hold values from -3 to 3
- w_in: bfloat16 [1024, 4096], P(None, 'chan'), may hold values from -0.1875 to 0.1875
- b_in: float32 [4096], P('chan'), may hold values from -3 to 3
- w_out: bfloat16 [4096, 1024], P('chan'), may hold values from -0.09375 to 0.09375
- layer_scale: float32 [1024], P('chan'), may hold values from 0.3 to 1.5
- group_sizes: int32 [4], replicated, may hold values from 1 to 4, 8 in all
Outputs:
- result: bfloat16 [8, 16, 64, 1024], P('dp', None, None, 'chan')
- d_input: bfloat16 [8, 16, 64, 1024], P('dp', None, None, 'chan')
- d_kernel: float32 [49, 1024], P(None, 'chan')
- d_gain: float32 [4, 1024], P(None, 'chan')
- d_bias: float32 [4, 1024], P(None, 'chan')
- d_w_in: float32 [1024, 4096], P('dp', 'chan')
- d_b_in: float32 [4096], P('chan')
- d_w_out: float32 [4096, 1024], P('chan', 'dp')
- d_scale: float32 [1024], P('chan')
Inputs may be any that keep to these rules, and one draw needn't show every extreme that they name: `group_sizes`: the sizes sum to 8, each is at least one, and the largest is exactly 4.
All inputs are finite; a program needn't handle non-finite values.
Results may differ from a plain program's by a relative error of at most 0.015.
Values may be sent and summed in bfloat16 or wider, within the bound.
A program may use at most 128 MiB of HBM per device.

v0:
```python
import jax
import jax.numpy as jnp
from jax import lax
from jax.sharding import PartitionSpec as P

KS = 7
EPS = 1e-05


def depthwise(field, kernel):
    reach = KS // 2
    height, width = (field.shape[1], field.shape[2])
    padded = jnp.pad(field, ((0, 0), (reach, reach), (reach, reach), (0, 0)))
    running = jnp.zeros(field.shape, jnp.float32)
    for shift_row in range(KS):
        for shift_col in range(KS):
            window = padded[:, shift_row : shift_row + height, shift_col : shift_col + width, :]
            running = running + window * kernel[shift_row * KS + shift_col]
    return running


def kernel_grad(field, upstream):
    reach = KS // 2
    height, width = (field.shape[1], field.shape[2])
    padded = jnp.pad(field, ((0, 0), (reach, reach), (reach, reach), (0, 0)))
    collected = []
    for shift_row in range(KS):
        for shift_col in range(KS):
            window = padded[:, shift_row : shift_row + height, shift_col : shift_col + width, :]
            collected.append(jnp.sum(window * upstream, axis=(0, 1, 2)))
    return jnp.stack(collected)


def group_owners(group_sizes, number):
    group_ends = jnp.cumsum(group_sizes)
    positions = jnp.arange(number, dtype=jnp.int32)
    labels = jnp.sum((group_ends[None, :] <= positions[:, None]).astype(jnp.int32), axis=1)
    return (jnp.arange(group_sizes.shape[0], dtype=jnp.int32)[:, None] == labels[None, :]).astype(
        jnp.float32
    )


def body(
    activations,
    cotangent,
    dw_kernel,
    norm_gain,
    norm_bias,
    w_in,
    b_in,
    w_out,
    layer_scale,
    group_sizes,
):
    height, width, channels = (activations.shape[1], activations.shape[2], activations.shape[3])
    row_count = height * width
    devices = lax.axis_size("dp")
    position = lax.axis_index("dp")
    group_ends = jnp.cumsum(group_sizes)
    own_group = jnp.sum((group_ends <= position).astype(jnp.int32))
    member = (jnp.arange(group_sizes.shape[0], dtype=jnp.int32) == own_group).astype(jnp.float32)
    counts = group_sizes.astype(jnp.float32) * row_count
    own_count = jnp.sum(member * counts)
    source = activations.astype(jnp.float32)
    filtered = depthwise(source, dw_kernel).reshape(row_count, channels)
    moments = jnp.stack([jnp.sum(filtered, axis=0), jnp.sum(filtered * filtered, axis=0)])
    per_device = lax.all_gather(moments[None], "dp", axis=0, tiled=True)
    owners = group_owners(group_sizes, devices)
    totals = jnp.sum(owners[:, :, None, None] * per_device[None], axis=1)
    group_mean = totals[:, 0] / counts[:, None]
    group_var = totals[:, 1] / counts[:, None] - group_mean * group_mean
    group_rstd = lax.rsqrt(group_var + EPS)
    own_mean = jnp.sum(member[:, None] * group_mean, axis=0)
    own_rstd = jnp.sum(member[:, None] * group_rstd, axis=0)
    own_gain = jnp.sum(member[:, None] * norm_gain, axis=0)
    own_bias = jnp.sum(member[:, None] * norm_bias, axis=0)
    centered = (filtered - own_mean) * own_rstd
    normed = (centered * own_gain + own_bias).astype(jnp.bfloat16)
    gathered = lax.all_gather(normed, "chan", axis=1, tiled=True)
    hidden = jnp.dot(gathered, w_in, preferred_element_type=jnp.float32) + b_in
    activated = jax.nn.gelu(hidden).astype(jnp.bfloat16)
    partial_branch = jnp.dot(activated, w_out, preferred_element_type=jnp.float32)
    branch = lax.psum_scatter(
        partial_branch.astype(jnp.bfloat16), "chan", scatter_dimension=1, tiled=True
    ).astype(jnp.float32)
    initial = source.reshape(row_count, channels)
    result = (initial + layer_scale * branch).astype(jnp.bfloat16).reshape(activations.shape)
    incoming = cotangent.reshape(row_count, channels).astype(jnp.float32)
    scale_local = jnp.sum(incoming * branch, axis=0)
    d_branch = (incoming * layer_scale).astype(jnp.bfloat16)
    branch_full = lax.all_gather(d_branch, "chan", axis=1, tiled=True)
    contract_rows = (((0,), (0,)), ((), ()))
    contract_cols = (((1,), (1,)), ((), ()))
    out_local_t = lax.dot_general(
        branch_full, activated, contract_rows, preferred_element_type=jnp.float32
    )
    d_activated = lax.dot_general(
        branch_full, w_out, contract_cols, preferred_element_type=jnp.float32
    )
    _, pullback = jax.vjp(jax.nn.gelu, hidden)
    d_hidden = pullback(d_activated)[0]
    bias_local = jnp.sum(d_hidden, axis=0)
    hidden_b = d_hidden.astype(jnp.bfloat16)
    in_local = lax.dot_general(
        gathered, hidden_b, contract_rows, preferred_element_type=jnp.float32
    )
    hidden_cols = in_local.shape[1]
    both_local = jnp.concatenate([in_local, out_local_t], axis=1)
    both_sums = lax.psum_scatter(
        both_local.astype(jnp.bfloat16), "dp", scatter_dimension=0, tiled=True
    ).astype(jnp.float32)
    d_w_in = both_sums[:, :hidden_cols]
    d_w_out = both_sums[:, hidden_cols:].T
    partial_normed = lax.dot_general(
        hidden_b, w_in, contract_cols, preferred_element_type=jnp.float32
    )
    d_normed = lax.psum_scatter(
        partial_normed.astype(jnp.bfloat16), "chan", scatter_dimension=1, tiled=True
    ).astype(jnp.float32)
    grad_moments = jnp.stack([jnp.sum(d_normed * centered, axis=0), jnp.sum(d_normed, axis=0)])
    grad_rows = lax.all_gather(grad_moments[None], "dp", axis=0, tiled=True)
    grad_owners = group_owners(group_sizes, devices)
    grad_totals = jnp.sum(grad_owners[:, :, None, None] * grad_rows[None], axis=1)
    d_gain = grad_totals[:, 0]
    d_bias = grad_totals[:, 1]
    own_dgain = jnp.sum(member[:, None] * d_gain, axis=0)
    own_dbias = jnp.sum(member[:, None] * d_bias, axis=0)
    d_filtered = (
        own_gain * own_rstd * (d_normed - own_dbias / own_count - centered * own_dgain / own_count)
    )
    d_filtered = d_filtered.reshape(activations.shape)
    kernel_local = kernel_grad(source, d_filtered)
    d_kernel, d_b_in, d_scale = lax.psum((kernel_local, bias_local, scale_local), "dp")
    d_input = (cotangent.astype(jnp.float32) + depthwise(d_filtered, dw_kernel[::-1])).astype(
        jnp.bfloat16
    )
    return (result, d_input, d_kernel, d_gain, d_bias, d_w_in, d_b_in, d_w_out, d_scale)


def solution(mesh):
    in_specs = (
        P("dp", None, None, "chan"),
        P("dp", None, None, "chan"),
        P(None, "chan"),
        P(None, "chan"),
        P(None, "chan"),
        P(None, "chan"),
        P("chan"),
        P("chan", None),
        P("chan"),
        P(),
    )
    out_specs = (
        P("dp", None, None, "chan"),
        P("dp", None, None, "chan"),
        P(None, "chan"),
        P(None, "chan"),
        P(None, "chan"),
        P("dp", "chan"),
        P("chan"),
        P("chan", "dp"),
        P("chan"),
    )
    return jax.shard_map(body, mesh=mesh, in_specs=in_specs, out_specs=out_specs, check_vma=False)
```

profile of v0, /device:TPU:0, one launch (start us, length us, event | category | flops | bytes accessed | tf_op | source)
XLA Modules:
  0.0 303.6 jit_solution(11111486553160216814)
XLA Ops:
  7.3 1.0 reduce-window.8
  8.2 0.6 fusion.117
  8.9 0.6 compare_convert_fusion.1
  9.5 1.9 fusion.116
  11.4 0.9 fusion.124
  12.4 1.1 fusion.122
  13.4 1.1 fusion.123
  14.6 0.1 convert_reduce_fusion.1
  14.7 1.1 convert_element_type.75
  15.8 9.7 %fusion.118 = (f32[256]{0:T(256)S(1)}, f32[256]{0:T(256)S(1)}, f32[1,16,64,256]{3,2,1,0:T(8,128)}) fusion(f32[256]{0:T(256)S(1)} %bitcast.229, f32[256]{0:T(256)S(1)} %bitcast.231, f32[256]{0:T(256)S(1)} %bitcast.235, f32[256]{0:T(256)S(1)} %bitcast.237, f32[256]{0:T(256)S(1)} %bitcast.239, f32[256]{0:T(256)S(1)} %bitcast.241, f32[256]{0:T(256)S(1)} %bitcast.243, ...), kind=kLoop, calls=%fused_computation.304 | loop fusion | flops 26213888 | bytes 2149376 | tf_op jit(solution)/shard_map/reduce_sum | solution.py:66
  25.5 27.9 %all-gather.2 = f32[8,2,256]{2,1,0:T(2,128)S(1)} all-gather(f32[1,2,256]{2,1,0:T(2,128)S(1)} %maximum_bitcast_fusion), channel_id=2, replica_groups=mesh['dp'=8,'chan'=4] {'dp'}, dimensions={0}, use_global_device_ids=true | all-gather | bytes 18432 | tf_op jit(solution)/shard_map/all_gather | solution.py:67
  53.5 0.1 multiply_reduce_fusion.51
  53.6 0.1 multiply_reduce_fusion.57
  53.7 2.2 add_convert_fusion
  55.9 0.0 reduce-scatter.6.cloned.1.call-start
  56.0 22.3 %all-gather.7.cloned.1.call-done = bf16[1024,1024]{1,0:T(8,128)(2,1)} async-done(((bf16[1024,256]{1,0:T(8,128)(2,1)}), bf16[1024,1024]{1,0:T(8,128)(2,1)}) %all-gather.7.cloned.1.call-update) | async-done | bytes 2097168 | tf_op jit(solution)/shard_map/all_gather | solution.py:79
  78.3 4.6 %fusion.127 = f32[1024,1024]{1,0:T(8,128)S(1)} fusion(bf16[1024,1024]{1,0:T(8,128)(2,1)} %all-gather.7.cloned.1.call-done, bf16[1024,1024]{1,0:T(8,128)(2,1)} %param.15), kind=kOutput, calls=%fused_computation.311 | convolution fusion | flops 2147483648 | bytes 8388608 | tf_op jit(solution)/shard_map/dot_general | solution.py:80
  82.8 1.9 copy-done.10
  84.8 4.2 %convolution_convert_fusion.3 = bf16[1024,1024]{1,0:T(8,128)(2,1)} fusion(bf16[1024,1024]{1,0:T(8,128)(2,1)S(1)} %copy-done, f32[1024,1024]{1,0:T(8,128)S(1)} %fusion.127, f32[1024]{0:T(1024)S(1)} %copy-done.9), kind=kOutput, calls=%fused_computation.109 | convolution fusion | flops 2159017984 | bytes 8392704 | tf_op jit(solution)/shard_map/dot_general | solution.py:82
  89.0 0.0 all-gather.9.cloned.1.call-start
  89.0 31.3 %reduce-scatter.6.cloned.1.call-done = bf16[1024,256]{1,0:T(8,128)(2,1)} async-done(((bf16[1024,1024]{1,0:T(8,128)(2,1)}), bf16[1024,256]{1,0:T(8,128)(2,1)}) %reduce-scatter.6.cloned.1.call-update) | async-done | bytes 524304 | tf_op jit(solution)/shard_map/reduce_scatter | solution.py:83
  120.3 2.7 fusion.8
  123.0 0.2 reduce-scatter.8.cloned.1.call-start
  123.2 22.7 %all-gather.9.cloned.1.call-done = bf16[1024,1024]{1,0:T(8,128)(2,1)} async-done(((bf16[1024,256]{1,0:T(8,128)(2,1)}), bf16[1024,1024]{1,0:T(8,128)(2,1)}) %all-gather.9.cloned.1.call-update) | async-done | bytes 2097168 | tf_op jit(solution)/shard_map/all_gather | solution.py:91
  145.9 7.5 %fusion.119 = (f32[1024]{0:T(1024)S(1)}, bf16[1024,1024]{1,0:T(8,128)(2,1)S(1)}) fusion(f32[1024,1024]{1,0:T(8,128)} %copy-done.10, f32[1024]{0:T(1024)S(1)} %copy-done.9, bf16[1024,1024]{1,0:T(8,128)(2,1)} %all-gather.9.cloned.1.call-done, bf16[1024,1024]{1,0:T(8,128)(2,1)S(1)} %copy-done), kind=kOutput, calls=%fused_computation.305 | convolution fusion | flops 2170551296 | bytes 10493952 | tf_op jit(solution)/shard_map/dot_general | solution.py:97
  153.4 1.3 copy-done.12
  154.7 3.8 %convolution_convert_fusion.2 = bf16[1024,1024]{1,0:T(8,128)(2,1)} fusion(bf16[1024,1024]{1,0:T(8,128)(2,1)S(1)} %copy-done.7, bf16[1024,1024]{1,0:T(8,128)(2,1)S(1)} %get-tuple-element.99), kind=kOutput, calls=%fused_computation.108 | convolution fusion | flops 2148532224 | bytes 6291456 | tf_op jit(solution)/shard_map/dot_general | solution.py:114
  158.5 0.0 reduce-scatter.10.cloned.1.call-start
  158.6 4.8 %convolution_convert_fusion.1 = bf16[1024,1024]{0,1:T(8,128)(2,1)S(1)} fusion(bf16[1024,1024]{1,0:T(8,128)(2,1)} %all-gather.7.cloned.1.call-done, bf16[1024,1024]{1,0:T(8,128)(2,1)} %copy-done.12), kind=kOutput, calls=%fused_computation.107 | convolution fusion | flops 2148532224 | bytes 6291456 | tf_op jit(solution)/shard_map/dot_general | solution.py:104
  163.4 3.0 convolution_convert_fusion
  166.4 2.4 pad_maximum_fusion
  168.8 6.5 %copy.27 = bf16[1024,2048]{1,0:T(8,128)(2,1)} copy(bf16[1024,2048]{0,1:T(8,128)(2,1)} %pad_maximum_fusion) | data formatting | bytes 8388608
  175.3 14.5 %reduce-scatter.8.cloned.1.call-done = bf16[1024,256]{1,0:T(8,128)(2,1)} async-done(((bf16[1024,1024]{1,0:T(8,128)(2,1)}), bf16[1024,256]{1,0:T(8,128)(2,1)}) %reduce-scatter.8.cloned.1.call-update) | async-done | bytes 524304 | tf_op jit(solution)/shard_map/reduce_scatter | solution.py:117
  189.8 1.7 fusion.9
  191.6 27.2 %all-gather.3 = f32[8,2,256]{2,1,0:T(2,128)S(1)} all-gather(f32[1,2,256]{2,1,0:T(2,128)S(1)} %maximum_bitcast_fusion.1), channel_id=3, replica_groups=mesh['dp'=8,'chan'=4] {'dp'}, dimensions={0}, use_global_device_ids=true | all-gather | bytes 18432 | tf_op jit(solution)/shard_map/all_gather | solution.py:121
  218.8 0.1 multiply_reduce_fusion.50
  218.9 0.6 multiply_reduce_fusion.53
  219.5 0.7 broadcast_divide_fusion
  220.2 4.5 %multiply_reduce_fusion.1 = (f32[256]{0:T(256)S(1)}, f32[256]{0:T(256)S(1)}, f32[256]{0:T(256)S(1)}, f32[256]{0:T(256)S(1)}, f32[256]{0:T(256)S(1)}, /*index=5*/...) fusion(f32[1,16,64,256]{3,2,1,0:T(8,128)S(1)} %convert_element_, ...), kind=kLoop, calls=%fused_computation.224 | loop fusion | flops 11529728 | bytes 3693572 | tf_op jit(solution)/shard_map/reduce_sum | solution.py:30
  224.7 1.6 multiply_reduce_fusion.2
  226.3 2.3 multiply_reduce_fusion
  228.6 0.2 stack.223
  228.8 36.8 %all-reduce.2 = (f32[49,256]{1,0:T(8,128)}, f32[1024]{0:T(1024)}, f32[256]{0:T(256)}) all-reduce(f32[49,256]{1,0:T(8,128)S(1)} %stack.223, f32[1024]{0:T(1024)S(1)} %get-tuple-element.98, f32[256]{0:T(256)S(1)} %get-tuple-element.104), channel_id=1, replica_groups=mesh['dp'=8,'chan'=4] {'dp'}, use_global_device_ids=true, to_apply=%region_67.68 | all-reduce | flops 13824 | bytes 110592 | tf_op jit(solution)/shard_map/psum | solution.py:133
  265.6 26.2 %fusion.106 = bf16[1,16,64,256]{3,2,1,0:T(8,128)(2,1)} fusion(f32[1,16,64,256]{3,2,1,0:T(8,128)} %bitcast.209, bf16[1,16,64,256]{3,2,1,0:T(8,128)(2,1)} %param.11, f32[256]{0:T(256)S(1)} %bitcast.230, f32[256]{0:T(256)S(1)} %bitcast.232, f32[256]{0:T(256)S(1)} %bitcast.236, f32[256]{0:T(256)S(1)} %bitcast.238, f32[256]{0:T(256)S(1)} %bitcast.240, ...), kind=kLoop, calls=%fused_computation.215 | loop fusion | flops 26214400 | bytes 2147328 | tf_op jit(solution)/shard_map/convert_element_type | solution.py:134
  291.8 1.3 copy.28
  293.2 1.1 convert_element_type.94
  294.2 1.0 copy.26
  295.2 1.9 slice_bitcast_fusion
  (40 shorter events, 0.3 us)
Async XLA Ops:
  7.2 77.6 %copy-start = (bf16[1024,1024]{1,0:T(8,128)(2,1)S(1)}, bf16[1024,1024]{1,0:T(8,128)(2,1)}, u32[]{:S(2)}) copy-start(bf16[1024,1024]{1,0:T(8,128)(2,1)} %param.17) | copy-start | bytes 6291460
  7.2 46.4 %copy-start.5 = (f32[4,256]{1,0:T(4,128)S(1)}, f32[4,256]{1,0:T(4,128)}, u32[]{:S(2)}) copy-start(f32[4,256]{1,0:T(4,128)} %param.14) | copy-start | bytes 12292
  7.2 46.4 %copy-start.4 = (f32[4,256]{1,0:T(4,128)S(1)}, f32[4,256]{1,0:T(4,128)}, u32[]{:S(2)}) copy-start(f32[4,256]{1,0:T(4,128)} %param.13) | copy-start | bytes 12292
  7.2 71.1 %all-gather.7.cloned.1.call-start = ((), (), s32[]{:S(2)}) async-start(), calls=%async_computation.3 | async-start | bytes 2621440 | tf_op jit(solution)/shard_map/all_gather | solution.py:79
  55.9 28.9 %copy-start.9 = (f32[1024]{0:T(1024)S(1)}, f32[1024]{0:T(1024)}, u32[]{:S(2)}) copy-start(f32[1024]{0:T(1024)} %param.16) | copy-start | bytes 12292
  55.9 64.4 %reduce-scatter.6.cloned.1.call-start = ((), (), s32[]{:S(2)}) async-start(), calls=%async_computation.4 | async-start | bytes 2621440 | tf_op jit(solution)/shard_map/reduce_scatter | solution.py:83
  82.8 1.9 copy-start.10
  88.9 31.3 %copy-start.6 = (f32[256]{0:T(256)S(1)}, f32[256]{0:T(256)}, u32[]{:S(2)}) copy-start(f32[256]{0:T(256)} %param.18) | copy-start | bytes 3076
  89.0 57.0 %all-gather.9.cloned.1.call-start = ((), (), s32[]{:S(2)}) async-start(), calls=%async_computation.5 | async-start | bytes 2621440 | tf_op jit(solution)/shard_map/all_gather | solution.py:91
  123.0 66.9 %reduce-scatter.8.cloned.1.call-start = ((), (), s32[]{:S(2)}) async-start(), calls=%async_computation.6 | async-start | bytes 2621440 | tf_op jit(solution)/shard_map/reduce_scatter | solution.py:117
  145.9 8.8 %copy-start.7 = (bf16[1024,1024]{1,0:T(8,128)(2,1)S(1)}, bf16[1024,1024]{1,0:T(8,128)(2,1)}, u32[]{:S(2)}) copy-start(bf16[1024,1024]{1,0:T(8,128)(2,1)} %param.15) | copy-start | bytes 6291460
  153.4 1.3 copy-start.12
  158.5 133.3 %reduce-scatter.10.cloned.1.call-start = ((), (), s32[]{:S(2)}) async-start(), calls=%async_computation.7 | async-start | bytes 4718592
  158.6 4.8 %copy-start.8 = (bf16[1024,1024]{1,0:T(8,128)(2,1)S(1)}, bf16[1024,1024]{1,0:T(8,128)(2,1)}, u32[]{:S(2)}) copy-start(bf16[1024,1024]{1,0:T(8,128)(2,1)} %all-gather.9.cloned.1.call-done) | copy-start | bytes 6291460
  158.6 4.8 %copy-start.11 = (f32[1024,1024]{1,0:T(8,128)S(1)}, f32[1024,1024]{1,0:T(8,128)}, u32[]{:S(2)}) copy-start(f32[1024,1024]{1,0:T(8,128)} %copy-done.10) | copy-start | bytes 12582916
  189.8 30.3 %copy-start.1 = (f32[1,16,64,256]{3,2,1,0:T(8,128)S(1)}, f32[1,16,64,256]{3,2,1,0:T(8,128)}, u32[]{:S(2)}) copy-start(f32[1,16,64,256]{3,2,1,0:T(8,128)} %get-tuple-element.103) | copy-start | bytes 3145732
  191.5 33.1 %copy-start.3 = (bf16[1,16,64,256]{3,2,1,0:T(8,128)(2,1)S(1)}, bf16[1,16,64,256]{3,2,1,0:T(8,128)(2,1)}, u32[]{:S(2)}) copy-start(bf16[1,16,64,256]{3,2,1,0:T(8,128)(2,1)} %param.10) | copy-start | bytes 1572868
  224.6 3.9 %copy-start.2 = (f32[1024,256]{1,0:T(8,128)}, f32[1024,256]{1,0:T(8,128)S(1)}, u32[]{:S(2)}) copy-start(f32[1024,256]{1,0:T(8,128)S(1)} %get-tuple-element.100) | copy-start | bytes 3145732
Sparse Core Ops, SparseCore 0:
  56.0 22.2 all-gather.6
  89.1 31.1 reduce-scatter.5
  123.1 22.8 all-gather.8
  158.6 31.1 reduce-scatter.7
  193.3 89.9 reduce-scatter.9
where the time goes:
time: 304 us
  blocking collectives  91.9 us (30%)
  waiting for transfers between devices  90.9 us (30%)
  other arithmetic  61.3 us (20%)
  matrix products  27.7 us (9%)
  local copies, waits for them, and re-layouts  17.3 us (6%)
  between operations  14.1 us (5%)
    psum x1, blocking collectives, body(): lax.psum((kernel_local, bias_local, scale_local), 'dp')  36.8 us
    reduce_scatter x1, waiting for transfers between devices, body(): lax.psum_scatter(partial_branch.astype(jnp.bfloat16), 'chan', scatter_dim...  31.3 us
    all_gather x1, blocking collectives, body(): per_device = lax.all_gather(moments[None], 'dp', axis=0, tiled=True)  27.9 us
    all_gather x1, blocking collectives, body(): grad_rows = lax.all_gather(grad_moments[None], 'dp', axis=0, tiled=True)  27.2 us
    convert_element_type x1, other arithmetic, body(): (cotangent.astype(jnp.float32) + depthwise(d_filtered, dw_kernel[::-1]))....  26.2 us
    all_gather x1, waiting for transfers between devices, body(): branch_full = lax.all_gather(d_branch, 'chan', axis=1, tiled=True)  22.7 us
    all_gather x1, waiting for transfers between devices, body(): gathered = lax.all_gather(normed, 'chan', axis=1, tiled=True)  22.3 us
    reduce_scatter x1, waiting for transfers between devices, body(): lax.psum_scatter(partial_normed.astype(jnp.bfloat16), 'chan', scatter_dim...  14.5 us
  transfers between devices with their start and end apart: 5, of which 4 were waited for; matrix products, arithmetic and copies ran while one was open for 18% of the time, Pallas kernels for 0%

commit v1 on v0

--- a/solution.py
+++ b/solution.py
@@ -88,7 +88,7 @@
     incoming = cotangent.reshape(row_count, channels).astype(jnp.float32)
     scale_local = jnp.sum(incoming * branch, axis=0)
     d_branch = (incoming * layer_scale).astype(jnp.bfloat16)
-    branch_full = lax.all_gather(d_branch, "chan", axis=1, tiled=True)
+    branch_full = jnp.concatenate(lax.all_gather(d_branch, "chan"), axis=1)
     contract_rows = (((0,), (0,)), ((), ()))
     contract_cols = (((1,), (1,)), ((), ()))
     out_local_t = lax.dot_general(

time: 304 us -> 263 us (0.87)
  waiting for transfers between devices: 90.9 us -> 58.7 us
  other arithmetic: 61.3 us -> 46.5 us
    unnamed x6, waiting for transfers between devices: 0.1 us -> 33 us
    reduce_scatter x1, waiting for transfers between devices: 31.3 us -> 0.01 us  [body(): lax.psum_scatter(partial_branch.astype(jnp.bfloat16), 'chan', scatter_dim...]
    all_gather x1, waiting for transfers between devices: 22.7 us -> 0.02 us  [body(): branch_full = jnp.concatenate(lax.all_gather(d_branch, 'chan'), axis=1)]
    convert_element_type x1, other arithmetic: 26.2 us -> 10.5 us  [body(): (cotangent.astype(jnp.float32) + depthwise(d_filtered, dw_kernel[::-1]))....]
    reduce_scatter x1, waiting for transfers between devices: 14.5 us -> 7.43 us  [body(): lax.psum_scatter(partial_normed.astype(jnp.bfloat16), 'chan', scatter_dim...]
    all_gather x1, waiting for transfers between devices: 22.3 us -> 18.3 us  [body(): gathered = lax.all_gather(normed, 'chan', axis=1, tiled=True)]
    all_gather x0 -> x1, local copies, waits for them, and re-layouts: none -> 4.01 us  [body(): branch_full = jnp.concatenate(lax.all_gather(d_branch, 'chan'), axis=1)]
    unnamed x29 -> x37, local copies, waits for them, and re-layouts: 12.1 us -> 10.2 us
  transfers between devices with their start and end apart: 5 -> 5, of which waited for: 4 -> 3; matrix products, arithmetic and copies ran while one was open for 18% -> 28% of each run, Pallas kernels for 0% -> 0%
where the time goes in v1:
time: 263 us; the launch traced here: 262 us
  blocking collectives  93.5 us (36%)
  waiting for transfers between devices  58.7 us (22%)
  other arithmetic  46.5 us (18%)
  matrix products  28.7 us (11%)
  local copies, waits for them, and re-layouts  20.2 us (8%)
  between operations  14.1 us (5%)
    psum x1, blocking collectives, body(): lax.psum((kernel_local, bias_local, scale_local), 'dp')  39.1 us
    unnamed x6, waiting for transfers between devices  33 us
    all_gather x1, blocking collectives, body(): per_device = lax.all_gather(moments[None], 'dp', axis=0, tiled=True)  27.9 us
    all_gather x1, blocking collectives, body(): grad_rows = lax.all_gather(grad_moments[None], 'dp', axis=0, tiled=True)  26.5 us
    all_gather x1, waiting for transfers between devices, body(): gathered = lax.all_gather(normed, 'chan', axis=1, tiled=True)  18.3 us
    convert_element_type x1, other arithmetic, body(): (cotangent.astype(jnp.float32) + depthwise(d_filtered, dw_kernel[::-1]))....  10.5 us
    unnamed x37, local copies, waits for them, and re-layouts  10.2 us
    reduce_sum x1, other arithmetic, body(): jnp.sum(filtered, axis=0)  9.63 us
  transfers between devices with their start and end apart: 5, of which 3 were waited for; matrix products, arithmetic and copies ran while one was open for 28% of the time, Pallas kernels for 0%

profile of v1, /device:TPU:0, one launch (start us, length us, event | category | flops | bytes accessed | tf_op | source)
XLA Modules:
  0.0 262.1 jit_solution(14346223415651264861)
XLA Ops:
  7.2 0.0 all-gather.9.cloned.1.call-start
  7.2 2.1 fusion.110
  9.4 0.0 all-gather.7.cloned.1.call-start
  9.5 1.0 fusion.122
  10.5 1.1 convert_element_type.94
  11.7 9.6 %fusion.118 = (f32[256]{0:T(256)S(1)}, f32[256]{0:T(256)S(1)}, f32[1,16,64,256]{3,2,1,0:T(8,128)}) fusion(f32[256]{0:T(256)S(1)} %bitcast.273, f32[256]{0:T(256)S(1)} %bitcast.275, f32[256]{0:T(256)S(1)} %bitcast.219, f32[256]{0:T(256)S(1)} %bitcast.221, f32[256]{0:T(256)S(1)} %bitcast.223, f32[256]{0:T(256)S(1)} %bitcast.225, f32[256]{0:T(256)S(1)} %bitcast.227, ...), kind=kLoop, calls=%fused_computation.304 | loop fusion | flops 26213888 | bytes 2149376 | tf_op jit(solution)/shard_map/reduce_sum | solution.py:66
  21.4 27.9 %all-gather.2 = f32[8,2,256]{2,1,0:T(2,128)S(1)} all-gather(f32[1,2,256]{2,1,0:T(2,128)S(1)} %maximum_bitcast_fusion), channel_id=2, replica_groups=mesh['dp'=8,'chan'=4] {'dp'}, dimensions={0}, use_global_device_ids=true | all-gather | bytes 18432 | tf_op jit(solution)/shard_map/all_gather | solution.py:67
  49.3 0.2 reduce-window.8
  49.5 0.6 fusion.117
  50.1 0.6 compare_convert_fusion.1
  50.8 0.1 convert_reduce_fusion.1
  50.8 0.1 multiply_reduce_fusion.51
  50.9 1.2 fusion.116
  52.2 0.1 multiply_reduce_fusion.57
  52.3 2.2 add_convert_fusion
  54.5 0.0 reduce-scatter.8.cloned.1.call-start
  54.6 0.0 all-gather.9.cloned.1.call-done
  54.6 4.0 %copy.28 = bf16[4,1024,256]{1,2,0:T(8,128)(2,1)} copy(bf16[4,1024,256]{2,1,0:T(8,128)(2,1)} %all-gather.9.cloned.1.call-done) | data formatting | bytes 4194304 | tf_op jit(solution)/shard_map/all_gather | solution.py:91
  58.6 18.3 %all-gather.7.cloned.1.call-done = bf16[1024,1024]{1,0:T(8,128)(2,1)} async-done(((bf16[1024,256]{1,0:T(8,128)(2,1)}), bf16[1024,1024]{1,0:T(8,128)(2,1)}) %all-gather.7.cloned.1.call-update) | async-done | bytes 2097168 | tf_op jit(solution)/shard_map/all_gather | solution.py:79
  76.9 4.7 %fusion.127 = f32[1024,1024]{1,0:T(8,128)S(1)} fusion(bf16[1024,1024]{1,0:T(8,128)(2,1)} %all-gather.7.cloned.1.call-done, bf16[1024,1024]{1,0:T(8,128)(2,1)} %param.15), kind=kOutput, calls=%fused_computation.311 | convolution fusion | flops 2147483648 | bytes 8388608 | tf_op jit(solution)/shard_map/dot_general | solution.py:80
  81.7 5.8 %fusion.119 = (f32[1024]{0:T(1024)}, bf16[1024,1024]{1,0:T(8,128)(2,1)S(1)}) fusion(f32[1024,1024]{1,0:T(8,128)S(1)} %fusion.127, f32[1024]{0:T(1024)S(1)} %copy-done.13, bf16[1024,1024]{0,1:T(8,128)(2,1)S(1)} %bitcast.214, bf16[1024,1024]{1,0:T(8,128)(2,1)S(1)} %copy-done), kind=kOutput, calls=%fused_computation.305 | convolution fusion | flops 2170551296 | bytes 10493952 | tf_op jit(solution)/shard_map/dot_general | solution.py:97
  87.4 1.4 copy-done.16
  88.8 3.7 %convolution_convert_fusion.2 = bf16[1024,1024]{1,0:T(8,128)(2,1)} fusion(bf16[1024,1024]{1,0:T(8,128)(2,1)S(1)} %copy-done.12, bf16[1024,1024]{1,0:T(8,128)(2,1)S(1)} %get-tuple-element.117), kind=kOutput, calls=%fused_computation.108 | convolution fusion | flops 2148532224 | bytes 6291456 | tf_op jit(solution)/shard_map/dot_general | solution.py:114
  92.5 0.2 reduce-scatter.6.cloned.1.call-start
  92.7 6.4 %convolution_convert_fusion.3 = bf16[1024,1024]{1,0:T(8,128)(2,1)} fusion(bf16[1024,1024]{1,0:T(8,128)(2,1)S(1)} %copy-done, f32[1024,1024]{1,0:T(8,128)} %copy-done.14, f32[1024]{0:T(1024)S(1)} %copy-done.13), kind=kOutput, calls=%fused_computation.109 | convolution fusion | flops 2159017984 | bytes 8392704 | tf_op jit(solution)/shard_map/dot_general | solution.py:82
  99.2 0.0 reduce-scatter.10.cloned.1.call-start
  99.2 5.2 %convolution_convert_fusion.1 = bf16[1024,1024]{0,1:T(8,128)(2,1)S(1)} fusion(bf16[1024,1024]{1,0:T(8,128)(2,1)} %all-gather.7.cloned.1.call-done, bf16[1024,1024]{1,0:T(8,128)(2,1)} %copy-done.16), kind=kOutput, calls=%fused_computation.107 | convolution fusion | flops 2148532224 | bytes 6291456 | tf_op jit(solution)/shard_map/dot_general | solution.py:104
  104.4 3.0 %convolution_convert_fusion = bf16[1024,1024]{0,1:T(8,128)(2,1)S(1)} fusion(bf16[1024,1024]{0,1:T(8,128)(2,1)S(1)} %bitcast.215, f32[1024,1024]{1,0:T(8,128)S(1)} %copy-done.15, f32[1024]{0:T(1024)S(1)} %copy-done.13), kind=kOutput, calls=%fused_computation.106 | convolution fusion | flops 2159017984 | bytes 8392704 | tf_op jit(solution)/shard_map/dot_general | solution.py:94
  107.4 2.4 pad_maximum_fusion
  109.9 6.5 %copy.33 = bf16[1024,2048]{1,0:T(8,128)(2,1)} copy(bf16[1024,2048]{0,1:T(8,128)(2,1)} %pad_maximum_fusion) | data formatting | bytes 8388608
  116.4 7.4 %reduce-scatter.8.cloned.1.call-done = bf16[1024,256]{1,0:T(8,128)(2,1)} async-done(((bf16[1024,1024]{1,0:T(8,128)(2,1)}), bf16[1024,256]{1,0:T(8,128)(2,1)}) %reduce-scatter.8.cloned.1.call-update) | async-done | bytes 524304 | tf_op jit(solution)/shard_map/reduce_scatter | solution.py:117
  123.8 1.7 fusion.9
  125.6 26.5 %all-gather.3 = f32[8,2,256]{2,1,0:T(2,128)S(1)} all-gather(f32[1,2,256]{2,1,0:T(2,128)S(1)} %maximum_bitcast_fusion.1), channel_id=3, replica_groups=mesh['dp'=8,'chan'=4] {'dp'}, dimensions={0}, use_global_device_ids=true | all-gather | bytes 18432 | tf_op jit(solution)/shard_map/all_gather | solution.py:121
  152.1 0.1 multiply_reduce_fusion.50
  152.2 0.6 multiply_reduce_fusion.53
  152.8 0.6 broadcast_divide_fusion
  153.5 4.5 %multiply_reduce_fusion.1 = (f32[256]{0:T(256)S(1)}, f32[256]{0:T(256)S(1)}, f32[256]{0:T(256)S(1)}, f32[256]{0:T(256)S(1)}, f32[256]{0:T(256)S(1)}, /*index=5*/...) fusion(f32[1,16,64,256]{3,2,1,0:T(8,128)S(1)} %convert_element_, ...), kind=kLoop, calls=%fused_computation.224 | loop fusion | flops 11529728 | bytes 3693572 | tf_op jit(solution)/shard_map/reduce_sum | solution.py:30
  158.0 2.2 multiply_reduce_fusion.2
  160.2 2.3 multiply_reduce_fusion
  162.5 2.9 %stack.223 = f32[49,256]{1,0:T(8,128)S(1)} concatenate(f32[1,256]{1,0:T(1,128)} %bitcast.361, f32[1,256]{1,0:T(1,128)} %bitcast.360, f32[1,256]{1,0:T(1,128)} %bitcast.362, f32[1,256]{1,0:T(1,128)S(1)} %bitcast.316, f32[1,256]{1,0:T(1,128)S(1)} %bitcast.317, f32[1,256]{1,0:T(1,128)S(1)} %bitcast.318, f32[1,256]{1,0:T(1,128)S(1)} %bitcast.319, f32[1,256]{1,0:T(1,128)S(1)} %bitcast.320, ...), dimensions={0} | concatenate | bytes 100352 | tf_op jit(solution)/shard_map/stack | solution.py:31
  165.5 2.4 fusion.8
  167.9 39.1 %all-reduce.2 = (f32[49,256]{1,0:T(8,128)}, f32[1024]{0:T(1024)}, f32[256]{0:T(256)}) all-reduce(f32[49,256]{1,0:T(8,128)S(1)} %stack.223, f32[1024]{0:T(1024)} %get-tuple-element.116, f32[256]{0:T(256)S(1)} %get-tuple-element.122), channel_id=1, replica_groups=mesh['dp'=8,'chan'=4] {'dp'}, use_global_device_ids=true, to_apply=%region_67.68 | all-reduce | flops 13824 | bytes 110592 | tf_op jit(solution)/shard_map/psum | solution.py:133
  207.0 10.5 %fusion.106 = bf16[1,16,64,256]{3,2,1,0:T(8,128)(2,1)} fusion(f32[1,16,64,256]{3,2,1,0:T(8,128)S(1)} %bitcast.213, f32[256]{0:T(256)S(1)} %bitcast.274, f32[256]{0:T(256)S(1)} %bitcast.276, f32[256]{0:T(256)S(1)} %bitcast.220, f32[256]{0:T(256)S(1)} %bitcast.222, f32[256]{0:T(256)S(1)} %bitcast.224, f32[256]{0:T(256)S(1)} %bitcast.226, ...), kind=kLoop, calls=%fused_computation.215 | loop fusion | flops 26214400 | bytes 2147328 | tf_op jit(solution)/shard_map/convert_element_type | solution.py:134
  217.4 32.9 %reduce-scatter.10.cloned.1.call-done = bf16[128,2048]{1,0:T(8,128)(2,1)} async-done(((bf16[1024,2048]{1,0:T(8,128)(2,1)}), bf16[128,2048]{1,0:T(8,128)(2,1)}) %reduce-scatter.10.cloned.1.call-update) | async-done | bytes 524304
  250.3 1.3 copy.34
  251.7 1.1 convert_element_type.113
  252.7 1.0 copy.32
  253.7 1.9 slice_bitcast_fusion
  (50 shorter events, 0.3 us)
Async XLA Ops:
  7.2 74.4 %copy-start = (bf16[1024,1024]{1,0:T(8,128)(2,1)S(1)}, bf16[1024,1024]{1,0:T(8,128)(2,1)}, u32[]{:S(2)}) copy-start(bf16[1024,1024]{1,0:T(8,128)(2,1)} %param.17) | copy-start | bytes 6291460
  7.2 4.5 %copy-start.7 = (f32[49,256]{1,0:T(8,128)S(1)}, f32[49,256]{1,0:T(8,128)}, u32[]{:S(2)}) copy-start(f32[49,256]{1,0:T(8,128)} %param.12) | copy-start | bytes 150532
  7.2 47.4 %all-gather.9.cloned.1.call-start = ((), (), s32[]{:S(2)}) async-start(), calls=%async_computation.5 | async-start | bytes 2621440 | tf_op jit(solution)/shard_map/all_gather | solution.py:91
  9.4 39.9 %copy-start.11 = (s32[4]{0:T(128)S(1)}, s32[4]{0:T(128)}, u32[]{:S(2)}) copy-start(s32[4]{0:T(128)} %param.19) | copy-start | bytes 52
  9.4 42.8 %copy-start.9 = (f32[4,256]{1,0:T(4,128)S(1)}, f32[4,256]{1,0:T(4,128)}, u32[]{:S(2)}) copy-start(f32[4,256]{1,0:T(4,128)} %param.13) | copy-start | bytes 12292
  9.4 42.8 %copy-start.10 = (f32[4,256]{1,0:T(4,128)S(1)}, f32[4,256]{1,0:T(4,128)}, u32[]{:S(2)}) copy-start(f32[4,256]{1,0:T(4,128)} %param.14) | copy-start | bytes 12292
  9.4 67.5 %all-gather.7.cloned.1.call-start = ((), (), s32[]{:S(2)}) async-start(), calls=%async_computation.3 | async-start | bytes 2621440 | tf_op jit(solution)/shard_map/all_gather | solution.py:79
  54.5 69.3 %reduce-scatter.8.cloned.1.call-start = ((), (), s32[]{:S(2)}) async-start(), calls=%async_computation.6 | async-start | bytes 2621440 | tf_op jit(solution)/shard_map/reduce_scatter | solution.py:117
  58.6 23.0 %copy-start.13 = (f32[1024]{0:T(1024)S(1)}, f32[1024]{0:T(1024)}, u32[]{:S(2)}) copy-start(f32[1024]{0:T(1024)} %param.16) | copy-start | bytes 12292
  76.9 4.7 %copy-start.5 = (bf16[4,1024,256]{1,2,0:T(8,128)(2,1)S(1)}, bf16[4,1024,256]{1,2,0:T(8,128)(2,1)}, u32[]{:S(2)}) copy-start(bf16[4,1024,256]{1,2,0:T(8,128)(2,1)} %copy.28) | copy-start | bytes 6291460
  81.6 5.8 %copy-start.14 = (f32[1024,1024]{1,0:T(8,128)}, f32[1024,1024]{1,0:T(8,128)S(1)}, u32[]{:S(2)}) copy-start(f32[1024,1024]{1,0:T(8,128)S(1)} %fusion.127) | copy-start | bytes 12582916
  81.7 7.1 %copy-start.12 = (bf16[1024,1024]{1,0:T(8,128)(2,1)S(1)}, bf16[1024,1024]{1,0:T(8,128)(2,1)}, u32[]{:S(2)}) copy-start(bf16[1024,1024]{1,0:T(8,128)(2,1)} %param.15) | copy-start | bytes 6291460
  87.4 1.4 copy-start.16
  92.5 73.0 %reduce-scatter.6.cloned.1.call-start = ((), (), s32[]{:S(2)}) async-start(), calls=%async_computation.4 | async-start | bytes 2621440 | tf_op jit(solution)/shard_map/reduce_scatter | solution.py:83
  99.2 151.2 %reduce-scatter.10.cloned.1.call-start = ((), (), s32[]{:S(2)}) async-start(), calls=%async_computation.7 | async-start | bytes 4718592
  99.2 5.2 %copy-start.6 = (bf16[4,1024,256]{1,2,0:T(8,128)(2,1)S(1)}, bf16[4,1024,256]{1,2,0:T(8,128)(2,1)}, u32[]{:S(2)}) copy-start(bf16[4,1024,256]{1,2,0:T(8,128)(2,1)} %copy.28) | copy-start | bytes 6291460
  99.2 5.2 %copy-start.15 = (f32[1024,1024]{1,0:T(8,128)S(1)}, f32[1024,1024]{1,0:T(8,128)}, u32[]{:S(2)}) copy-start(f32[1024,1024]{1,0:T(8,128)} %copy-done.14) | copy-start | bytes 12582916
  123.8 29.7 %copy-start.1 = (f32[1,16,64,256]{3,2,1,0:T(8,128)S(1)}, f32[1,16,64,256]{3,2,1,0:T(8,128)}, u32[]{:S(2)}) copy-start(f32[1,16,64,256]{3,2,1,0:T(8,128)} %get-tuple-element.121) | copy-start | bytes 3145732
  125.5 32.4 %copy-start.4 = (bf16[1,16,64,256]{3,2,1,0:T(8,128)(2,1)S(1)}, bf16[1,16,64,256]{3,2,1,0:T(8,128)(2,1)}, u32[]{:S(2)}) copy-start(bf16[1,16,64,256]{3,2,1,0:T(8,128)(2,1)} %param.10) | copy-start | bytes 1572868
  158.0 4.5 %copy-start.2 = (f32[1024,256]{1,0:T(8,128)}, f32[1024,256]{1,0:T(8,128)S(1)}, u32[]{:S(2)}) copy-start(f32[1024,256]{1,0:T(8,128)S(1)} %get-tuple-element.118) | copy-start | bytes 3145732
  158.0 7.5 %copy-start.8 = (f32[256]{0:T(256)S(1)}, f32[256]{0:T(256)}, u32[]{:S(2)}) copy-start(f32[256]{0:T(256)} %param.18) | copy-start | bytes 3076
  162.5 44.5 %copy-start.3 = (f32[1024,256]{1,0:T(8,128)S(1)}, f32[1024,256]{1,0:T(8,128)}, u32[]{:S(2)}) copy-start(f32[1024,256]{1,0:T(8,128)} %copy-done.2) | copy-start | bytes 3145732
Sparse Core Ops, SparseCore 0:
  10.1 25.2 all-gather.8
  54.7 22.2 all-gather.6
  92.6 31.1 reduce-scatter.7
  126.2 31.1 reduce-scatter.5
  160.9 89.4 reduce-scatter.9
